TPU v7x, 32 devices: a whole 2x2x4 slice. The times are simulated.
32 devices in a mesh: wide: 8 (over z, y), narrow: 4 (over x, core).
Axes of the slice: x: 2, y: 2, z: 4, core: 2. Of those that a mesh axis runs over, the one named last changes fastest.
Arguments:
- solution: float32 [8, 16384], P(None, ('wide', 'narrow')), may hold values from -6 to 6
- residual: float32 [8, 16384], P(None, ('wide', 'narrow')), may hold values from -600 to 600
- direction: float32 [8, 16384], P(None, ('wide', 'narrow')), may hold values from -600 to 600
- error_var: float32 [16384], P(('wide', 'narrow')), may hold values from 0.25 to 2
- footprint: bfloat16 [16384, 4, 128], P(('wide', 'narrow')), may hold values from -0.25 to 0.25
- tiles: int32 [16384, 4], P(('wide', 'narrow')), may hold values from 0 to 1279
- window: int32 [16384, 1], P(('wide', 'narrow')), may hold values from 0 to 7; in each aligned block of 512 rows (0 to 511, 512 to 1023, ...) at most 160 rows name the same one
- temporal: bfloat16 [320, 320], replicated, may hold values from -40 to 40, as said below
- spatial_lat: bfloat16 [128, 128], replicated, may hold values from -40 to 40, as said below
- spatial_lon: bfloat16 [128, 128], replicated, may hold values from -40 to 40, as said below
Outputs:
- solution_new: float32 [8, 16384], P(None, ('wide', 'narrow'))
- residual_new: float32 [8, 16384], P(None, ('wide', 'narrow'))
- direction_new: float32 [8, 16384], P(None, ('wide', 'narrow'))
Inputs may be any that keep to these rules, and one draw needn't show every extreme that they name: At most 160 of the observations held by one device share a window, and some device reaches that in every draw. `temporal`: A symmetric positive definite covariance. `spatial_lat`: A symmetric positive definite covariance. `spatial_lon`: A symmetric positive definite covariance.
All inputs are finite; a program needn't handle non-finite values.
Results may differ from a plain program's by a relative error of at most 0.004.
Values may be sent and summed in bfloat16 or wider, within the bound.
A program may use at most 128 MiB of HBM per device.

v0:
```python
import math

import jax
import jax.numpy as jnp
from jax import lax
from jax.sharding import PartitionSpec as P

HIGHEST = lax.Precision.HIGHEST


def chol_solve(matrix, right):
    chol_low = jnp.linalg.cholesky(matrix)
    half_solve = lax.linalg.triangular_solve(chol_low, right, left_side=True, lower=True)
    return lax.linalg.triangular_solve(
        chol_low, half_solve, left_side=True, lower=True, transpose_a=True
    )


def gram_matrix(left, right):
    return jnp.dot(left, right.T, precision=HIGHEST)


def on_device(
    solution,
    residual,
    direction,
    error_var,
    footprint,
    tiles,
    window,
    temporal,
    spatial_lat,
    spatial_lon,
):
    n_wide = lax.axis_size("wide")
    n_narrow = lax.axis_size("narrow")
    rhs_count, obs_dev = direction.shape
    days_total = temporal.shape[0]
    day_dev = days_total // n_wide
    lat_total = spatial_lat.shape[0]
    lat_band = lat_total // n_narrow
    lon_count = spatial_lon.shape[0]
    tile_count = tiles.shape[1]
    capacity = obs_dev * 5 // (2 * n_wide)
    slot_total = n_wide * capacity
    tiles_local = day_dev * lat_band
    window_id = window[:, 0]
    dir_half = direction.astype(jnp.bfloat16)
    matches = (window_id[:, None] == jnp.arange(n_wide, dtype=jnp.int32)[None, :]).astype(jnp.int32)
    before = jnp.cumsum(matches, axis=0) - matches
    position = jnp.sum(before * matches, axis=1)
    slot_index = window_id * capacity + position
    source = (
        jnp.full((slot_total,), obs_dev, jnp.int32)
        .at[slot_index]
        .set(jnp.arange(obs_dev, dtype=jnp.int32))
    )
    foot_rows = jnp.concatenate(
        [
            footprint.reshape(obs_dev, tile_count * lon_count),
            jnp.zeros((1, tile_count * lon_count), jnp.bfloat16),
        ],
        0,
    )
    dir_rows = jnp.concatenate([dir_half.T, jnp.zeros((1, rhs_count), jnp.bfloat16)], 0)
    tile_rows = jnp.concatenate([tiles, jnp.zeros((1, tile_count), jnp.int32)], 0)
    recv_foot, recv_dir, recv_tiles = (
        lax.all_to_all(
            foot_rows[source].reshape(n_wide, capacity, tile_count * lon_count),
            "wide",
            split_axis=0,
            concat_axis=0,
            tiled=True,
        ),
        lax.all_to_all(
            dir_rows[source].reshape(n_wide, capacity, rhs_count),
            "wide",
            split_axis=0,
            concat_axis=0,
            tiled=True,
        ),
        lax.all_to_all(
            tile_rows[source].reshape(n_wide, capacity, tile_count),
            "wide",
            split_axis=0,
            concat_axis=0,
            tiled=True,
        ),
    )
    block_size = math.gcd(slot_total, 128)
    block_count = slot_total // block_size
    rows_block = block_size * tile_count
    foot_blocks = recv_foot.reshape(block_count, rows_block, lon_count)
    dir_blocks = jnp.repeat(recv_dir.reshape(slot_total, rhs_count), tile_count, axis=0).reshape(
        block_count, rows_block, rhs_count
    )
    id_blocks = recv_tiles.reshape(block_count, rows_block)
    tile_range = jnp.arange(tiles_local, dtype=jnp.int32)

    def adjoint_step(accum, inputs):
        foot_block, dir_block, id_block = inputs
        onehot = (id_block[None, :] == tile_range[:, None]).astype(jnp.bfloat16)
        weighted = (onehot[:, None, :] * dir_block.T[None, :, :]).reshape(
            tiles_local * rhs_count, rows_block
        )
        return (accum + jnp.dot(weighted, foot_block, preferred_element_type=jnp.float32), None)

    start_accum = jnp.zeros((tiles_local * rhs_count, lon_count), jnp.float32)
    accum, _ = lax.scan(adjoint_step, start_accum, (foot_blocks, dir_blocks, id_blocks))
    flat_flux = accum.astype(jnp.bfloat16).reshape(day_dev, lat_band * rhs_count * lon_count)
    all_days = lax.all_to_all(flat_flux, "wide", split_axis=1, concat_axis=0, tiled=True)
    mixed_days = jnp.dot(temporal, all_days, preferred_element_type=jnp.float32).astype(
        jnp.bfloat16
    )
    timed_flux = lax.all_to_all(mixed_days, "wide", split_axis=0, concat_axis=1, tiled=True)
    timed_flux = timed_flux.reshape(day_dev, lat_band, rhs_count, lon_count)
    narrow_index = lax.axis_index("narrow")
    lat_rows = lax.dynamic_slice_in_dim(spatial_lat, narrow_index * lat_band, lat_band, 0)
    lat_sum = jnp.einsum(
        "ab,dbrl->darl",
        lat_rows,
        lax.all_gather(timed_flux, "narrow", axis=1, tiled=True),
        preferred_element_type=jnp.float32,
    )
    spread_lat = lat_sum.astype(jnp.bfloat16)
    smoothed = jnp.dot(
        spread_lat.reshape(-1, lon_count), spatial_lon.T, preferred_element_type=jnp.float32
    ).astype(jnp.bfloat16)
    flux_table = smoothed.reshape(tiles_local, rhs_count * lon_count)

    def forward_step(accum_dummy, inputs):
        foot_block, id_block = inputs
        picked = flux_table[id_block].reshape(rows_block, rhs_count, lon_count)
        return (
            accum_dummy,
            jnp.einsum("jrl,jl->jr", picked, foot_block, preferred_element_type=jnp.float32),
        )

    _, model_rows = lax.scan(forward_step, jnp.zeros((), jnp.float32), (foot_blocks, id_blocks))
    back_rows = (
        model_rows.reshape(slot_total, tile_count, rhs_count)
        .sum(axis=1)
        .reshape(n_wide, capacity, rhs_count)
    )
    home_rows = lax.all_to_all(back_rows, "wide", split_axis=0, concat_axis=0, tiled=True).reshape(
        slot_total, rhs_count
    )
    model_part = home_rows[slot_index].T
    model_image = model_part + error_var[None, :] * direction
    curvature, res_norm = lax.psum(
        (gram_matrix(direction, model_image), gram_matrix(residual, residual)), ("wide", "narrow")
    )
    sym = 0.5 * (curvature + curvature.T)
    step_matrix = chol_solve(sym, res_norm)
    residual_new = residual - jnp.dot(step_matrix.T, model_image, precision=HIGHEST)
    norm_new = lax.psum(gram_matrix(residual_new, residual_new), ("wide", "narrow"))
    solution_new = solution + jnp.dot(step_matrix.T, direction, precision=HIGHEST)
    ratio_matrix = chol_solve(res_norm, norm_new)
    direction_new = residual_new + jnp.dot(ratio_matrix.T, direction, precision=HIGHEST)
    return (solution_new, residual_new, direction_new)


def solution(mesh):
    in_specs = (
        P(None, ("wide", "narrow")),
        P(None, ("wide", "narrow")),
        P(None, ("wide", "narrow")),
        P(("wide", "narrow")),
        P(("wide", "narrow"), None, None),
        P(("wide", "narrow"), None),
        P(("wide", "narrow"), None),
        P(),
        P(),
        P(),
    )
    out_specs = (
        P(None, ("wide", "narrow")),
        P(None, ("wide", "narrow")),
        P(None, ("wide", "narrow")),
    )
    return jax.shard_map(
        on_device, mesh=mesh, in_specs=in_specs, out_specs=out_specs, check_vma=False
    )
```

profile of v0, /device:TPU:0, one launch (start us, length us, event | category | flops | bytes accessed | tf_op | source)
XLA Modules:
  0.0 548.3 jit_solution(6296830245109133020)
XLA Ops:
  18.0 7.3 %all-to-all-start = ((s32[8,160,4]{1,2,0:T(4,128)}), s32[8,160,4]{1,2,0:T(4,128)S(1)}, u32[]{:S(2)}, u32[]{:S(2)}) async-start(s32[8,160,4]{1,2,0:T(4,128)} %copy.140), calls=%async_computation | async-start | bytes 65536 | tf_op jit(solution)/shard_map/all_to_all | solution.py:82
  29.2 2.9 all-to-all-done
  32.0 3.3 all-to-all-start.1
  35.5 4.7 gather_fusion.3
  42.0 4.2 all-to-all-start.2
  47.8 28.6 %all-to-all-done.2 = bf16[8,160,512]{2,1,0:T(8,128)(2,1)S(1)} async-done(((bf16[8,160,512]{2,1,0:T(8,128)(2,1)}), bf16[8,160,512]{2,1,0:T(8,128)(2,1)S(1)}, u32[]{:S(2)}, u32[]{:S(2)}) %all-to-all-start.2) | async-done | bytes 1310752 | tf_op jit(solution)/shard_map/all_to_all | solution.py:68
  77.3 68.1 %while.22 = (s32[]{:T(128)}, f32[10240,128]{1,0:T(8,128)}, s32[10,512]{1,0:T(8,128)S(1)}, bf16[10,512,8]{1,2,0:T(8,128)(2,1)S(1)}, bf16[10,512,128]{2,1,0:T(8,128)(2,1)S(1)}, /*index=5*/s32[]{:T(128)}, s32[]{:T(128)}) while((s32[]{:T(128)}, f32[10240,128]{1,0:T(8,128)}, s32[10,512]{1,0:T(8,128)S(1)}, ...), condition=%wide.region_5.6_spmd.clone, body=%wide.region_4.5_spmd.clone.sunk | while | flops 1351352320 | bytes 13269091 | solution.py:109
  77.9 4.7 convolution_add_fusion.4
  83.2 6.4 %convolution_add_fusion.4 = f32[10240,128]{1,0:T(8,128)} fusion(f32[10240,128]{1,0:T(8,128)} %get-tuple-element.209, bf16[8,512]{1,0:T(8,128)(2,1)S(1)} %dynamic-slice_bitcast_fusion.5, bf16[1280,512]{1,0:T(8,128)(2,1)S(1)} %fusion.68, pred[]{:T(512)S(6)} %compare.30, bf16[10,512,128]{2,1,0:T(8,128)(2,1)S(1)} %get-tuple-element.219, ...), kind=kOutput, calls=%fused_computation.13.clone.1 | convolution fusion | flops 1350041600 | bytes 11935749 | tf_op jit(solution)/shard_map/while/body/eval_jaxpr/dot_general | solution.py:106
  90.2 6.4 %convolution_add_fusion.4 = f32[10240,128]{1,0:T(8,128)} fusion(f32[10240,128]{1,0:T(8,128)} %get-tuple-element.209, bf16[8,512]{1,0:T(8,128)(2,1)S(1)} %dynamic-slice_bitcast_fusion.5, bf16[1280,512]{1,0:T(8,128)(2,1)S(1)} %fusion.68, pred[]{:T(512)S(6)} %compare.30, bf16[10,512,128]{2,1,0:T(8,128)(2,1)S(1)} %get-tuple-element.219, ...), kind=kOutput, calls=%fused_computation.13.clone.1 | convolution fusion | flops 1350041600 | bytes 11935749 | tf_op jit(solution)/shard_map/while/body/eval_jaxpr/dot_general | solution.py:106
  97.2 6.4 %convolution_add_fusion.4 = f32[10240,128]{1,0:T(8,128)} fusion(f32[10240,128]{1,0:T(8,128)} %get-tuple-element.209, bf16[8,512]{1,0:T(8,128)(2,1)S(1)} %dynamic-slice_bitcast_fusion.5, bf16[1280,512]{1,0:T(8,128)(2,1)S(1)} %fusion.68, pred[]{:T(512)S(6)} %compare.30, bf16[10,512,128]{2,1,0:T(8,128)(2,1)S(1)} %get-tuple-element.219, ...), kind=kOutput, calls=%fused_computation.13.clone.1 | convolution fusion | flops 1350041600 | bytes 11935749 | tf_op jit(solution)/shard_map/while/body/eval_jaxpr/dot_general | solution.py:106
  104.1 6.4 %convolution_add_fusion.4 = f32[10240,128]{1,0:T(8,128)} fusion(f32[10240,128]{1,0:T(8,128)} %get-tuple-element.209, bf16[8,512]{1,0:T(8,128)(2,1)S(1)} %dynamic-slice_bitcast_fusion.5, bf16[1280,512]{1,0:T(8,128)(2,1)S(1)} %fusion.68, pred[]{:T(512)S(6)} %compare.30, bf16[10,512,128]{2,1,0:T(8,128)(2,1)S(1)} %get-tuple-element.219, ...), kind=kOutput, calls=%fused_computation.13.clone.1 | convolution fusion | flops 1350041600 | bytes 11935749 | tf_op jit(solution)/shard_map/while/body/eval_jaxpr/dot_general | solution.py:106
  111.1 6.4 %convolution_add_fusion.4 = f32[10240,128]{1,0:T(8,128)} fusion(f32[10240,128]{1,0:T(8,128)} %get-tuple-element.209, bf16[8,512]{1,0:T(8,128)(2,1)S(1)} %dynamic-slice_bitcast_fusion.5, bf16[1280,512]{1,0:T(8,128)(2,1)S(1)} %fusion.68, pred[]{:T(512)S(6)} %compare.30, bf16[10,512,128]{2,1,0:T(8,128)(2,1)S(1)} %get-tuple-element.219, ...), kind=kOutput, calls=%fused_computation.13.clone.1 | convolution fusion | flops 1350041600 | bytes 11935749 | tf_op jit(solution)/shard_map/while/body/eval_jaxpr/dot_general | solution.py:106
  118.1 6.4 %convolution_add_fusion.4 = f32[10240,128]{1,0:T(8,128)} fusion(f32[10240,128]{1,0:T(8,128)} %get-tuple-element.209, bf16[8,512]{1,0:T(8,128)(2,1)S(1)} %dynamic-slice_bitcast_fusion.5, bf16[1280,512]{1,0:T(8,128)(2,1)S(1)} %fusion.68, pred[]{:T(512)S(6)} %compare.30, bf16[10,512,128]{2,1,0:T(8,128)(2,1)S(1)} %get-tuple-element.219, ...), kind=kOutput, calls=%fused_computation.13.clone.1 | convolution fusion | flops 1350041600 | bytes 11935749 | tf_op jit(solution)/shard_map/while/body/eval_jaxpr/dot_general | solution.py:106
  125.1 6.4 %convolution_add_fusion.4 = f32[10240,128]{1,0:T(8,128)} fusion(f32[10240,128]{1,0:T(8,128)} %get-tuple-element.209, bf16[8,512]{1,0:T(8,128)(2,1)S(1)} %dynamic-slice_bitcast_fusion.5, bf16[1280,512]{1,0:T(8,128)(2,1)S(1)} %fusion.68, pred[]{:T(512)S(6)} %compare.30, bf16[10,512,128]{2,1,0:T(8,128)(2,1)S(1)} %get-tuple-element.219, ...), kind=kOutput, calls=%fused_computation.13.clone.1 | convolution fusion | flops 1350041600 | bytes 11935749 | tf_op jit(solution)/shard_map/while/body/eval_jaxpr/dot_general | solution.py:106
  132.1 6.4 %convolution_add_fusion.4 = f32[10240,128]{1,0:T(8,128)} fusion(f32[10240,128]{1,0:T(8,128)} %get-tuple-element.209, bf16[8,512]{1,0:T(8,128)(2,1)S(1)} %dynamic-slice_bitcast_fusion.5, bf16[1280,512]{1,0:T(8,128)(2,1)S(1)} %fusion.68, pred[]{:T(512)S(6)} %compare.30, bf16[10,512,128]{2,1,0:T(8,128)(2,1)S(1)} %get-tuple-element.219, ...), kind=kOutput, calls=%fused_computation.13.clone.1 | convolution fusion | flops 1350041600 | bytes 11935749 | tf_op jit(solution)/shard_map/while/body/eval_jaxpr/dot_general | solution.py:106
  139.0 6.4 %convolution_add_fusion.4 = f32[10240,128]{1,0:T(8,128)} fusion(f32[10240,128]{1,0:T(8,128)} %get-tuple-element.209, bf16[8,512]{1,0:T(8,128)(2,1)S(1)} %dynamic-slice_bitcast_fusion.5, bf16[1280,512]{1,0:T(8,128)(2,1)S(1)} %fusion.68, pred[]{:T(512)S(6)} %compare.30, bf16[10,512,128]{2,1,0:T(8,128)(2,1)S(1)} %get-tuple-element.219, ...), kind=kOutput, calls=%fused_computation.13.clone.1 | convolution fusion | flops 1350041600 | bytes 11935749 | tf_op jit(solution)/shard_map/while/body/eval_jaxpr/dot_general | solution.py:106
  146.5 3.7 convert_element_type.38
  150.2 3.8 all_to_all.41
  155.5 62.7 %all_to_all.55 = bf16[40,8,4096]{2,0,1:T(8,128)(2,1)S(1)} all-to-all(bf16[40,8,4096]{2,0,1:T(8,128)(2,1)S(1)} %copy.147), channel_id=1, replica_groups=mesh['wide'=8,'narrow'=4] {'wide'}, dimensions={1} | all-to-all | bytes 5242880 | tf_op jit(solution)/shard_map/all_to_all | solution.py:111
  219.8 62.7 %all_to_all.56 = bf16[8,40,4096]{2,1,0:T(8,128)(2,1)S(1)} all-to-all(bf16[8,40,4096]{2,1,0:T(8,128)(2,1)S(1)} %bitcast.147), channel_id=1, replica_groups=mesh['wide'=8,'narrow'=4] {'wide'}, dimensions={0} | all-to-all | bytes 5242880 | tf_op jit(solution)/shard_map/all_to_all | solution.py:115
  283.9 3.2 reshape.167
  287.1 3.9 copy.149
  292.4 67.8 %all-gather.2.cloned.1.call-done = bf16[40,128,8,128]{3,1,2,0:T(8,128)(2,1)} async-done(((bf16[40,32,8,128]{3,1,2,0:T(8,128)(2,1)}), bf16[40,128,8,128]{3,1,2,0:T(8,128)(2,1)}) %all-gather.2.cloned.1.call-update) | async-done | bytes 10485776 | tf_op jit(solution)/shard_map/all_gather | solution.py:122
  360.2 5.5 %convert_bitcast_fusion = bf16[40,32,8,128]{3,1,2,0:T(8,128)(2,1)S(1)} fusion(bf16[40,128,8,128]{3,1,2,0:T(8,128)(2,1)} %all-gather.2.cloned.1.call-done, bf16[128,128]{1,0:T(8,128)(2,1)} %param.27, s32[]{:T(128)S(6)} %select_n.28), kind=kOutput, calls=%fused_computation.27 | convolution fusion | flops 336855040 | bytes 13115396 | tf_op jit(solution)/shard_map/ab,dbrl->darl/dot_general | solution.py:119
  369.3 3.8 reshape.169
  373.2 60.6 %while.21 = (s32[]{:T(128)}, f32[10,512,8]{1,2,0:T(8,128)S(1)}, s32[10,512]{1,0:T(8,128)S(1)}, bf16[1280,1024]{1,0:T(8,128)(2,1)S(1)}, bf16[10,512,128]{2,1,0:T(8,128)(2,1)}, /*index=5*/s32[]{:T(128)}) while((s32[]{:T(128)}, f32[10,512,8]{1,2,0:T(8,128)S(1)}, s32[10,512]{1,0:T(8,128)S(1)}, bf16[1280,1024]{1,0:T(8,128)(2,1)S(1)}, ...), condition=%wide.region_7.8_spmd, body=%wide.region_6.7_spmd.sunk | while | flops 1051138 | bytes 5730385 | solution.py:139
  434.6 5.4 reduce_sum.22
  441.0 5.5 %all-to-all-start.5 = ((f32[8,160,8]{1,2,0:T(8,128)}), f32[8,160,8]{1,2,0:T(8,128)S(1)}, u32[]{:S(2)}, u32[]{:S(2)}) async-start(f32[8,160,8]{1,2,0:T(8,128)} %copy.153), calls=%async_computation.5 | async-start | bytes 131072 | tf_op jit(solution)/shard_map/all_to_all | solution.py:145
  447.2 6.2 %all-to-all-done.5 = f32[8,160,8]{1,2,0:T(8,128)S(1)} async-done(((f32[8,160,8]{1,2,0:T(8,128)}), f32[8,160,8]{1,2,0:T(8,128)S(1)}, u32[]{:S(2)}, u32[]{:S(2)}) %all-to-all-start.5) | async-done | bytes 40992 | tf_op jit(solution)/shard_map/all_to_all | solution.py:145
  454.9 37.9 %all-reduce.3 = (f32[8,8]{0,1:T(8,128)S(1)}, f32[8,8]{1,0:T(8,128)S(1)}) all-reduce(f32[8,8]{0,1:T(8,128)S(1)} %copy-done.8, f32[8,8]{1,0:T(8,128)S(1)} %convolution_bitcast_fusion), channel_id=1, replica_groups=mesh['wide'=8,'narrow'=4] {'wide','narrow'}, use_global_device_ids=true, to_apply=%region_12.14 | all-reduce | flops 128 | bytes 1024 | tf_op jit(solution)/shard_map/psum | solution.py:150
  499.2 40.3 %psum.23 = f32[8,8]{1,0:T(8,128)S(1)} all-reduce(f32[8,8]{1,0:T(8,128)S(1)} %fusion.36), channel_id=1, replica_groups=mesh['wide'=8,'narrow'=4] {'wide','narrow'}, use_global_device_ids=true, to_apply=%region_13.17 | all-reduce | flops 64 | bytes 512 | tf_op jit(solution)/shard_map/psum | solution.py:156
  (204 shorter events, 107.7 us)
Async XLA Ops:
  7.2 211.1 %copy-start = (bf16[320,320]{1,0:T(8,128)(2,1)S(1)}, bf16[320,320]{1,0:T(8,128)(2,1)}, u32[]{:S(2)}) copy-start(bf16[320,320]{1,0:T(8,128)(2,1)} %param.26) | copy-start | bytes 614404
  10.8 0.6 copy-start.11
  14.7 10.6 %copy-start.3 = (f32[8,512]{1,0:T(8,128)S(1)}, f32[8,512]{1,0:T(8,128)}, u32[]{:S(2)}) copy-start(f32[8,512]{1,0:T(8,128)} %param.21) | copy-start | bytes 49156
  17.1 18.3 %copy-start.4 = (bf16[512,4,128]{2,1,0:T(4,128)(2,1)S(1)}, bf16[512,4,128]{2,1,0:T(4,128)(2,1)}, u32[]{:S(2)}) copy-start(bf16[512,4,128]{2,1,0:T(4,128)(2,1)} %param.23) | copy-start | bytes 1572868
  18.0 14.0 %all-to-all-start = ((s32[8,160,4]{1,2,0:T(4,128)}), s32[8,160,4]{1,2,0:T(4,128)S(1)}, u32[]{:S(2)}, u32[]{:S(2)}) async-start(s32[8,160,4]{1,2,0:T(4,128)} %copy.140), calls=%async_computation | async-start | bytes 65536 | tf_op jit(solution)/shard_map/all_to_all | solution.py:82
  32.0 10.0 %all-to-all-start.1 = ((bf16[8,160,8]{1,2,0:T(8,128)(2,1)}), bf16[8,160,8]{1,2,0:T(8,128)(2,1)S(1)}, u32[]{:S(2)}, u32[]{:S(2)}) async-start(bf16[8,160,8]{1,2,0:T(8,128)(2,1)} %copy.143), calls=%async_computation.1 | async-start | bytes 65536 | tf_op jit(solution)/shard_map/all_to_all | solution.py:75
  42.0 34.5 %all-to-all-start.2 = ((bf16[8,160,512]{2,1,0:T(8,128)(2,1)}), bf16[8,160,512]{2,1,0:T(8,128)(2,1)S(1)}, u32[]{:S(2)}, u32[]{:S(2)}) async-start(bf16[8,160,512]{2,1,0:T(8,128)(2,1)} %bitcast.17), calls=%async_computation.2 | async-start | bytes 2621440 | tf_op jit(solution)/shard_map/all_to_all | solution.py:68
  46.1 314.0 %all-gather.2.cloned.1.call-start = ((), (), s32[]{:S(2)}) async-start(), calls=%async_computation.6 | async-start | bytes 13107200 | tf_op jit(solution)/shard_map/all_gather | solution.py:122
  145.4 1.1 copy-start.2
  290.9 0.7 copy-start.6
  365.7 1.3 copy-start.7
  434.6 106.9 %copy-start.1 = (bf16[320,320]{1,0:T(8,128)(2,1)S(1)}, bf16[320,320]{1,0:T(8,128)(2,1)}, u32[]{:S(2)}) copy-start(bf16[320,320]{1,0:T(8,128)(2,1)} %param.26) | copy-start | bytes 614404
  440.0 14.8 %copy-start.10 = (f32[512]{0:T(512)S(1)}, f32[512]{0:T(512)}, u32[]{:S(2)}) copy-start(f32[512]{0:T(512)} %param.22) | copy-start | bytes 6148
  440.0 14.9 %copy-start.8 = (f32[8,8]{0,1:T(8,128)S(1)}, f32[8,8]{0,1:T(8,128)}, u32[]{:S(2)}) copy-start(f32[8,8]{0,1:T(8,128)} %fusion.35) | copy-start | bytes 772
  440.0 100.6 %copy-start.9 = (f32[8,512]{1,0:T(8,128)S(1)}, f32[8,512]{1,0:T(8,128)}, u32[]{:S(2)}) copy-start(f32[8,512]{1,0:T(8,128)} %param.19) | copy-start | bytes 49156
  441.0 12.4 %all-to-all-start.5 = ((f32[8,160,8]{1,2,0:T(8,128)}), f32[8,160,8]{1,2,0:T(8,128)S(1)}, u32[]{:S(2)}, u32[]{:S(2)}) async-start(f32[8,160,8]{1,2,0:T(8,128)} %copy.153), calls=%async_computation.5 | async-start | bytes 131072 | tf_op jit(solution)/shard_map/all_to_all | solution.py:145
  499.0 42.4 %copy-start.5 = (f32[8,512]{1,0:T(8,128)}, f32[8,512]{1,0:T(8,128)S(1)}, u32[]{:S(2)}) copy-start(f32[8,512]{1,0:T(8,128)S(1)} %convolution_subtract_fusion) | copy-start | bytes 49156
Sparse Core Ops, SparseCore 0:
  291.1 69.0 all-gather.1
where the time goes:
time: 550 us; the launch traced here: 548 us
  blocking collectives  204 us (37%)
  waiting for transfers between devices  107 us (19%)
  local copies, waits for them, and re-layouts  95.5 us (17%)
  matrix products  82.1 us (15%)
  other arithmetic  24.4 us (4%)
  starting transfers between devices  20.4 us (4%)
  between operations  14.4 us (3%)
    all_gather x1, waiting for transfers between devices, on_device(): lax.all_gather(timed_flux, 'narrow', axis=1, tiled=True)  67.8 us
    all_to_all x1, blocking collectives, on_device(): lax.all_to_all(flat_flux, 'wide', split_axis=1, concat_axis=0, tiled=True)  62.7 us
    all_to_all x1, blocking collectives, on_device(): lax.all_to_all(mixed_days, 'wide', split_axis=0, concat_axis=1, tiled=True)  62.7 us
    dot_general x10, matrix products, adjoint_step(): jnp.dot(weighted, foot_block, preferred_element_type=jnp.float32)  62.1 us
    psum x1, blocking collectives, on_device(): lax.psum(gram_matrix(residual_new, residual_new), ('wide', 'narrow'))  40.3 us
    psum x1, blocking collectives, on_device(): lax.psum((gram_matrix(direction, model_image), gram_matrix(residual, resi...  37.9 us
    all_to_all x1, waiting for transfers between devices, on_device(): lax.all_to_all(foot_rows[source].reshape(n_wide, capacity, tile_count * l...  28.6 us
    gather x10, local copies, waits for them, and re-layouts, forward_step(): picked = flux_table[id_block].reshape(rows_block, rhs_count, lon_count)  27.9 us
  transfers between devices with their start and end apart: 5, of which 5 were waited for; matrix products, arithmetic and copies ran while one was open for 2% of the time, Pallas kernels for 0%

commit v1 on v0

v1 whole, which is shorter than its diff:
```python
import functools

import jax
import jax.numpy as jnp
from jax import lax
from jax.experimental import pallas as pl
from jax.experimental.pallas import tpu as pltpu
from jax.sharding import PartitionSpec as P

HIGHEST = lax.Precision.HIGHEST
VMEM_LIMIT = 66 * 1000 * 1000
GROUP = 32


def chol_solve(matrix, right):
    chol_low = jnp.linalg.cholesky(matrix)
    half_solve = lax.linalg.triangular_solve(chol_low, right, left_side=True, lower=True)
    return lax.linalg.triangular_solve(
        chol_low, half_solve, left_side=True, lower=True, transpose_a=True
    )


def gram_matrix(left, right):
    return jnp.dot(left, right.T, precision=HIGHEST)


def adjoint_kernel(
    dims, cells, wins, me_ref, foot, dirs, equal, mix, out, picked, count, acc
):
    n_src, n_tiles, obs_dev, days, lat_band, rhs = dims
    lanes = foot.shape[-1]
    table_rows = acc.shape[0]
    chunk = 256

    @pl.loop(0, table_rows // chunk)
    def _(step):
        acc[pl.ds(pl.multiple_of(step * chunk, chunk), chunk), :] = jnp.zeros(
            (chunk, lanes), jnp.float32
        )

    me = me_ref[0]
    groups = obs_dev // GROUP

    def body(step, found):
        src = step // groups
        local = (step % groups) * GROUP
        base = src * obs_dev + local
        rows = [
            foot[
                pl.ds(pl.multiple_of((src * n_tiles + k) * obs_dev + local, GROUP), GROUP), :
            ].astype(jnp.float32)
            for k in range(n_tiles)
        ]
        same = equal[pl.ds(pl.multiple_of(base, GROUP), GROUP), :]
        sums = []
        pair = 0
        for k in range(n_tiles):
            total = rows[k]
            for m in range(k):
                total = total + same[:, pair : pair + 1] * rows[m]
                pair += 1
            sums.append(total)
        weights = dirs[step]
        for j in range(GROUP):
            weight = jnp.broadcast_to(weights[:, j : j + 1], (rhs, lanes))
            place = [
                pl.ds(pl.multiple_of(cells[(base + j) * n_tiles + k], rhs), rhs)
                for k in range(n_tiles)
            ]
            old = [acc[place[k], :] for k in range(n_tiles)]
            for k in range(n_tiles):
                acc[place[k], :] = old[k] + weight * sums[k][j : j + 1, :]
            picked[found] = base + j
            found = found + (wins[base + j] == me).astype(jnp.int32)
        return found

    count[0] = lax.fori_loop(0, n_src * groups, body, jnp.int32(0))

    @pl.loop(0, lat_band)
    def _(lat):
        for r in range(0, rhs, 2):
            both = jnp.concatenate(
                [
                    acc[pl.ds(lat * (days * rhs) + r + q, days, stride=rhs), :].astype(jnp.bfloat16)
                    for q in range(2)
                ],
                1,
            )
            mixed = jnp.dot(mix[...], both, preferred_element_type=jnp.float32)
            mixed = mixed.astype(out.dtype)
            out[lat * rhs + r] = mixed[:, :lanes]
            out[lat * rhs + r + 1] = mixed[:, lanes:]


def forward_kernel(dims, cells, picked, count, foot, spread, lon_t, out, wide_foot, table, parts):
    n_tiles, obs_dev, day_dev, rhs, group = dims
    lanes = foot.shape[-1]
    chunk = 256

    @pl.loop(0, foot.shape[0] // chunk)
    def _(step):
        block = pl.ds(pl.multiple_of(step * chunk, chunk), chunk)
        wide_foot[block, :] = foot[block, :].astype(jnp.float32)

    rows = table.shape[0]

    @pl.loop(0, rows // chunk)
    def _(step):
        block = pl.ds(pl.multiple_of(step * chunk, chunk), chunk)
        table[block, :] = (
            jnp.dot(spread[block, :], lon_t[...], preferred_element_type=jnp.float32)
            .astype(jnp.bfloat16)
            .astype(jnp.float32)
        )

    @pl.loop(0, out.shape[0] // chunk)
    def _(step):
        block = pl.ds(pl.multiple_of(step * chunk, chunk), chunk)
        out[block, :] = jnp.zeros((chunk, rhs), jnp.float32)

    total = count[0]

    @pl.loop(0, (total + group - 1) // group)
    def _(step):
        names = []
        for j in range(group):
            name = picked[jnp.minimum(step * group + j, total - 1)]
            names.append(name)
            first = name + (name // obs_dev) * ((n_tiles - 1) * obs_dev)
            value = None
            for k in range(n_tiles):
                cell = table[pl.ds(cells[name * n_tiles + k], rhs, stride=day_dev), :]
                row = wide_foot[pl.ds(first + k * obs_dev, 1), :]
                term = cell * row
                value = term if value is None else value + term
            parts[j] = value
        reduced = jnp.sum(parts[...], axis=-1)
        for j in range(group):
            out[pl.ds(names[j], 1), :] = reduced[j : j + 1, :]


def sum_kernel(n_wide, n_narrow, x_ref, out_ref, held, send_sem, recv_sem):
    count = n_wide * n_narrow
    me = lax.axis_index("wide") * n_narrow + lax.axis_index("narrow")
    barrier = pltpu.get_barrier_semaphore()

    def coords(who):
        return (who // n_narrow, who % n_narrow)

    @pl.loop(1, count)
    def _(step):
        pl.semaphore_signal(
            barrier,
            inc=1,
            device_id=coords((me + step) % count),
            device_id_type=pl.DeviceIdType.MESH,
        )

    pl.semaphore_wait(barrier, count - 1)

    def transfer(step):
        return pltpu.make_async_remote_copy(
            src_ref=x_ref,
            dst_ref=held.at[step],
            send_sem=send_sem.at[step],
            recv_sem=recv_sem.at[step],
            device_id=coords((me + step) % count),
            device_id_type=pl.DeviceIdType.MESH,
        )

    @pl.loop(1, count)
    def _(step):
        transfer(step).start()

    @pl.loop(1, count)
    def _(step):
        transfer(step).wait()

    held[0] = x_ref[...]

    def add(src, total):
        return total + held[(me - src + count) % count]

    out_ref[...] = lax.fori_loop(0, count, add, jnp.zeros(x_ref.shape, jnp.float32))


def sum_everywhere(x, n_wide, n_narrow, collective_id):
    count = n_wide * n_narrow
    rows, cols = x.shape
    padded = jnp.pad(x, ((0, 0), (0, 128 - cols)))
    return pl.pallas_call(
        functools.partial(sum_kernel, n_wide, n_narrow),
        out_shape=jax.ShapeDtypeStruct(padded.shape, jnp.float32),
        in_specs=[pl.BlockSpec(memory_space=pltpu.VMEM)],
        out_specs=pl.BlockSpec(memory_space=pltpu.VMEM),
        scratch_shapes=[
            pltpu.VMEM((count,) + padded.shape, jnp.float32),
            pltpu.SemaphoreType.DMA((count,)),
            pltpu.SemaphoreType.DMA((count,)),
        ],
        compiler_params=pltpu.CompilerParams(collective_id=collective_id, has_side_effects=True),
    )(padded)[:, :cols]


def on_device(
    solution,
    residual,
    direction,
    error_var,
    footprint,
    tiles,
    window,
    temporal,
    spatial_lat,
    spatial_lon,
):
    n_wide = lax.axis_size("wide")
    n_narrow = lax.axis_size("narrow")
    rhs, obs_dev = direction.shape
    days = temporal.shape[0]
    day_dev = days // n_wide
    lat_total = spatial_lat.shape[0]
    lat_band = lat_total // n_narrow
    lanes = spatial_lon.shape[0]
    n_tiles = tiles.shape[1]
    obs = n_wide * obs_dev
    wide_index = lax.axis_index("wide")
    narrow_index = lax.axis_index("narrow")
    smem = pl.BlockSpec(memory_space=pltpu.SMEM)
    vmem = pl.BlockSpec(memory_space=pltpu.VMEM)

    day_local, lat_local = tiles // lat_band, tiles % lat_band
    adjoint_cells = (lat_local * days + window * day_dev + day_local) * rhs
    forward_cells = lat_local * (rhs * day_dev) + day_local
    pairs = [(m, k) for k in range(n_tiles) for m in range(k)]
    equal = jnp.stack([(tiles[:, m] == tiles[:, k]) for m, k in pairs], 1).astype(jnp.int32)
    meta = jnp.concatenate(
        [adjoint_cells.reshape(-1), forward_cells.reshape(-1), window.reshape(-1), equal.reshape(-1)]
    )
    dir_half = direction.astype(jnp.bfloat16)
    floats = jnp.concatenate(
        [
            footprint.transpose(1, 0, 2).reshape(n_tiles * obs_dev, lanes),
            dir_half.reshape(rhs * obs_dev // lanes, lanes),
        ],
        0,
    )
    all_floats = lax.all_gather(floats, "wide", axis=0)
    all_meta = lax.all_gather(meta, "wide", axis=0)
    foot = all_floats[:, : n_tiles * obs_dev].reshape(n_wide * n_tiles * obs_dev, lanes)
    dirs = (
        all_floats[:, n_tiles * obs_dev :]
        .reshape(n_wide, rhs, obs_dev // GROUP, GROUP)
        .transpose(0, 2, 1, 3)
        .reshape(obs // GROUP, rhs, GROUP)
        .astype(jnp.float32)
    )
    cut = n_tiles * obs_dev
    cells_adj = all_meta[:, :cut].reshape(-1)
    cells_fwd = all_meta[:, cut : 2 * cut].reshape(-1)
    wins = all_meta[:, 2 * cut : 2 * cut + obs_dev].reshape(-1)
    same = all_meta[:, 2 * cut + obs_dev :].reshape(obs, len(pairs)).astype(jnp.float32)
    mix = lax.dynamic_slice_in_dim(temporal, wide_index * day_dev, day_dev, 0)

    timed, picked, count = pl.pallas_call(
        functools.partial(
            adjoint_kernel, (n_wide, n_tiles, obs_dev, days, lat_band, rhs)
        ),
        out_shape=(
            jax.ShapeDtypeStruct((lat_band * rhs, day_dev, lanes), jnp.bfloat16),
            jax.ShapeDtypeStruct((obs,), jnp.int32),
            jax.ShapeDtypeStruct((1,), jnp.int32),
        ),
        in_specs=[smem, smem, smem, vmem, vmem, vmem, vmem],
        out_specs=(vmem, smem, smem),
        scratch_shapes=[pltpu.VMEM((lat_band * days * rhs, lanes), jnp.float32)],
        compiler_params=pltpu.CompilerParams(vmem_limit_bytes=VMEM_LIMIT),
    )(cells_adj, wins, wide_index.reshape(1).astype(jnp.int32), foot, dirs, same, mix)

    gathered = lax.all_gather(
        timed.reshape(lat_band, rhs * day_dev * lanes), "narrow", axis=0, tiled=True
    )
    lat_rows = lax.dynamic_slice_in_dim(spatial_lat, narrow_index * lat_band, lat_band, 0)
    spread = jnp.dot(lat_rows, gathered, preferred_element_type=jnp.float32).astype(jnp.bfloat16)
    spread = spread.reshape(lat_band * rhs * day_dev, lanes)

    group = 16
    model = pl.pallas_call(
        functools.partial(forward_kernel, (n_tiles, obs_dev, day_dev, rhs, group)),
        out_shape=jax.ShapeDtypeStruct((obs, rhs), jnp.float32),
        in_specs=[smem, smem, smem, vmem, vmem, vmem],
        out_specs=vmem,
        scratch_shapes=[
            pltpu.VMEM((n_wide * n_tiles * obs_dev, lanes), jnp.float32),
            pltpu.VMEM((lat_band * rhs * day_dev, lanes), jnp.float32),
            pltpu.VMEM((group, rhs, lanes), jnp.float32),
        ],
        compiler_params=pltpu.CompilerParams(vmem_limit_bytes=VMEM_LIMIT),
    )(cells_fwd, picked, count, foot, spread, spatial_lon.T)

    home = lax.all_to_all(
        model.reshape(n_wide, obs_dev * rhs), "wide", split_axis=0, concat_axis=0, tiled=True
    )
    model_part = home.sum(axis=0).reshape(obs_dev, rhs).T
    model_image = model_part + error_var[None, :] * direction
    sums = sum_everywhere(
        jnp.concatenate(
            [gram_matrix(direction, model_image), gram_matrix(residual, residual)], 1
        ),
        n_wide,
        n_narrow,
        1,
    )
    curvature, res_norm = sums[:, :rhs], sums[:, rhs:]
    sym = 0.5 * (curvature + curvature.T)
    step_matrix = chol_solve(sym, res_norm)
    residual_new = residual - jnp.dot(step_matrix.T, model_image, precision=HIGHEST)
    norm_new = sum_everywhere(gram_matrix(residual_new, residual_new), n_wide, n_narrow, 2)
    solution_new = solution + jnp.dot(step_matrix.T, direction, precision=HIGHEST)
    ratio_matrix = chol_solve(res_norm, norm_new)
    direction_new = residual_new + jnp.dot(ratio_matrix.T, direction, precision=HIGHEST)
    return (solution_new, residual_new, direction_new)


def solution(mesh):
    split = ("wide", "narrow")
    in_specs = (
        P(None, split),
        P(None, split),
        P(None, split),
        P(split),
        P(split, None, None),
        P(split, None),
        P(split, None),
        P(),
        P(),
        P(),
    )
    out_specs = (P(None, split), P(None, split), P(None, split))
    return jax.shard_map(
        on_device, mesh=mesh, in_specs=in_specs, out_specs=out_specs, check_vma=False
    )
```

time: 550 us -> 319 us (0.58)
  blocking collectives: 204 us -> 33.7 us
  Pallas kernels: 0 us -> 107 us
  matrix products: 82.1 us -> 9.77 us
  local copies, waits for them, and re-layouts: 95.5 us -> 27 us
  starting transfers between devices: 20.4 us -> 3.45 us
  other arithmetic: 24.4 us -> 10.1 us
    all_to_all x2 -> x0, blocking collectives: 125 us -> none  [the longest x1 62.7 us: on_device(): lax.all_to_all(flat_flux, 'wide', split_axis=1, concat_axis=0, tiled=True)]
    pallas_call x0 -> x4, Pallas kernels: none -> 107 us  [the longest x1 61.8 us: on_device(): pl.pallas_call(functools.partial(adjoint_kernel, (n_wide, n_tiles, obs_de...]
    psum x2 -> x0, blocking collectives: 78.2 us -> none  [the longest x1 40.3 us: on_device(): lax.psum(gram_matrix(residual_new, residual_new), ('wide', 'narrow'))]
    dot_general x23 -> x1, matrix products: 78.5 us -> 5.49 us  [on_device(): jnp.dot(lat_rows, gathered, preferred_element_type=jnp.float32)]
    gather x15 -> x0, local copies, waits for them, and re-layouts: 38.9 us -> none  [the longest x10 27.9 us: forward_step(): picked = flux_table[id_block].reshape(rows_block, rhs_count, lon_count)]
    all_gather x1 -> x2, waiting for transfers between devices: 67.8 us -> 105 us  [the longest x1 67.4 us: on_device(): lax.all_gather(timed.reshape(lat_band, rhs * day_dev * lanes), 'narrow',...]
    all_gather x0 -> x1, blocking collectives: none -> 33.7 us  [on_device(): all_meta = lax.all_gather(meta, 'wide', axis=0)]
    all_to_all x4 -> x1, waiting for transfers between devices: 39.5 us -> 7.14 us  [on_device(): lax.all_to_all(model.reshape(n_wide, obs_dev * rhs), 'wide', split_axis=0...]
  transfers between devices with their start and end apart: 5 -> 3, of which waited for: 5 -> 3; matrix products, arithmetic and copies ran while one was open for 2% -> 2% of each run, Pallas kernels for 0% -> 0%
where the time goes in v1:
time: 319 us; the launch traced here: 318 us
  waiting for transfers between devices  112 us (35%)
  Pallas kernels  107 us (34%)
  blocking collectives  33.7 us (11%)
  local copies, waits for them, and re-layouts  27 us (8%)
  between operations  14.3 us (4%)
  other arithmetic  10.1 us (3%)
  matrix products  9.77 us (3%)
  starting transfers between devices  3.45 us (1%)
    all_gather x1, waiting for transfers between devices, on_device(): lax.all_gather(timed.reshape(lat_band, rhs * day_dev * lanes), 'narrow',...  67.4 us
    pallas_call x1, Pallas kernels, on_device(): pl.pallas_call(functools.partial(adjoint_kernel, (n_wide, n_tiles, obs_de...  61.8 us
    all_gather x1, waiting for transfers between devices, on_device(): all_floats = lax.all_gather(floats, 'wide', axis=0)  37.7 us
    all_gather x1, blocking collectives, on_device(): all_meta = lax.all_gather(meta, 'wide', axis=0)  33.7 us
    pallas_call x1, Pallas kernels, on_device(): pl.pallas_call(functools.partial(forward_kernel, (n_tiles, obs_dev, day_d...  24.5 us
    pallas_call x2, Pallas kernels, sum_everywhere(): pl.pallas_call(functools.partial(sum_kernel, n_wide, n_narrow), out_shape...  20.8 us
    all_to_all x1, waiting for transfers between devices, on_device(): lax.all_to_all(model.reshape(n_wide, obs_dev * rhs), 'wide', split_axis=0...  7.14 us
  transfers between devices with their start and end apart: 3, of which 3 were waited for; matrix products, arithmetic and copies ran while one was open for 2% of the time, Pallas kernels for 0%

profile of v1, /device:TPU:0, one launch (start us, length us, event | category | flops | bytes accessed | tf_op | source)
XLA Modules:
  0.0 317.8 jit_solution(9303264153453215650)
XLA Ops:
  7.2 1.1 copy.59
  8.4 0.7 convert_element_type.33
  9.1 0.9 pad_maximum_fusion
  11.2 33.7 %all-gather.2 = s32[8,1,7680]{2,1,0:T(1,128)S(1)} all-gather(s32[1,1,7680]{2,1,0:T(1,128)S(1)} %reshape.101), channel_id=2, replica_groups=mesh['wide'=8,'narrow'=4] {'wide'}, dimensions={0}, use_global_device_ids=true | all-gather | bytes 276480 | tf_op jit(solution)/shard_map/all_gather | solution.py:249
  45.7 3.5 %convert_element_type.39.equal = f32[4096,6]{1,0:T(8,128)} reshape(f32[8,3072]{1,0:T(8,128)S(1)} %slice_convert_fusion) | data formatting | bytes 196608 | tf_op jit(solution)/shard_map/convert_element_type | solution.py:262
  50.4 37.7 %all-gather.8.cloned.1.call-done = bf16[16640,128]{1,0:T(8,128)(2,1)} async-done(((bf16[2080,128]{1,0:T(8,128)(2,1)}), bf16[16640,128]{1,0:T(8,128)(2,1)}) %all-gather.8.cloned.1.call-update) | async-done | bytes 4259856 | tf_op jit(solution)/shard_map/all_gather | solution.py:248
  88.1 4.5 %slice.74 = bf16[8,2048,128]{2,1,0:T(8,128)(2,1)} slice(bf16[8,2080,128]{2,1,0:T(8,128)(2,1)} %bitcast.79), slice={[0:8], [0:2048], [0:128]} | slice | bytes 8388608 | tf_op jit(solution)/shard_map/slice | solution.py:250
  92.7 0.8 slice_convert_fusion.1
  93.7 1.0 copy.60
  94.7 61.8 %shard_map.121 = (bf16[256,40,128]{2,1,0:T(8,128)(2,1)}, s32[4096]{0:T(1024)}, s32[1]{0:T(128)}) custom-call(s32[16384]{0:T(1024)} %bitcast.86, s32[4096]{0:T(1024)} %bitcast.89, s32[1]{0:T(128)} %bitcast.2.me_ref, bf16[16384,128]{1,0:T(8,128)(2,1)} %bitcast.77, f32[128,8,32]{2,1,0:T(8,128)} %bitcast.81, f32[4096,6]{1,0:T(8,128)} %convert_element_type.39.equal, ...), custom_call_target="tpu_custom_call" | custom-call | tf_op jit(solution)/shard_map/pallas_call | solution.py:265
  156.5 4.5 %reshape.89 = bf16[32,40960]{1,0:T(8,128)(2,1)} reshape(bf16[256,40,128]{2,1,0:T(8,128)(2,1)} %get-tuple-element.11) | data formatting | bytes 5242880 | tf_op jit(solution)/shard_map/reshape | solution.py:281
  161.7 0.7 copy.61
  162.4 67.4 %all-gather.6.cloned.1.call-done = bf16[128,40960]{1,0:T(8,128)(2,1)} async-done(((bf16[32,40960]{1,0:T(8,128)(2,1)}), bf16[128,40960]{1,0:T(8,128)(2,1)}) %all-gather.6.cloned.1.call-update) | async-done | bytes 10485776 | tf_op jit(solution)/shard_map/all_gather | solution.py:280
  229.8 5.5 %convolution_convert_fusion = bf16[32,40960]{1,0:T(8,128)(2,1)S(1)} fusion(bf16[128,40960]{1,0:T(8,128)(2,1)} %all-gather.6.cloned.1.call-done, bf16[128,128]{1,0:T(8,128)(2,1)} %param.23, s32[]{:T(128)S(6)} %select_n.24), kind=kOutput, calls=%fused_computation | convolution fusion | flops 336855040 | bytes 13115396 | tf_op jit(solution)/shard_map/dot_general | solution.py:284
  235.3 2.6 reshape.90.spread
  237.9 24.5 %shard_map.122 = f32[4096,8]{1,0:T(8,128)} custom-call(s32[16384]{0:T(1024)} %bitcast.87, s32[4096]{0:T(1024)} %get-tuple-element.9.picked, s32[1]{0:T(128)} %get-tuple-element.10.count, bf16[16384,128]{1,0:T(8,128)(2,1)} %bitcast.78, bf16[10240,128]{1,0:T(8,128)(2,1)} %reshape.90.spread, bf16[128,128]{1,0:T(8,128)(2,1)} %bitcast.88), custom_call_target="tpu_custom_call" | custom-call | tf_op jit(solution)/shard_map/pallas_call | solution.py:288
  262.4 3.4 %all_to_all.8 = f32[8,1,4096]{2,1,0:T(1,128)} reshape(f32[4096,8]{1,0:T(8,128)} %shard_map.122) | data formatting | bytes 262144 | tf_op jit(solution)/shard_map/all_to_all | solution.py:301
  265.8 3.4 %all-to-all-start = ((f32[8,1,4096]{2,1,0:T(1,128)}), f32[8,1,4096]{2,1,0:T(1,128)S(1)}, u32[]{:S(2)}, u32[]{:S(2)}) async-start(f32[8,1,4096]{2,1,0:T(1,128)} %all_to_all.8), calls=%async_computation | async-start | bytes 262144 | tf_op jit(solution)/shard_map/all_to_all | solution.py:301
  269.3 7.1 %all-to-all-done = f32[8,1,4096]{2,1,0:T(1,128)S(1)} async-done(((f32[8,1,4096]{2,1,0:T(1,128)}), f32[8,1,4096]{2,1,0:T(1,128)S(1)}, u32[]{:S(2)}, u32[]{:S(2)}) %all-to-all-start) | async-done | bytes 131104 | tf_op jit(solution)/shard_map/all_to_all | solution.py:301
  277.0 0.7 select_maximum_fusion.x_ref
  277.7 10.8 %shard_map.123 = f32[8,128]{1,0:T(8,128)} custom-call(f32[8,128]{1,0:T(8,128)} %select_maximum_fusion.x_ref), custom_call_target="tpu_custom_call" | custom-call | tf_op jit(solution)/shard_map/pallas_call | solution.py:191
  288.5 0.7 slice.69
  289.3 0.8 fusion.15
  290.1 0.7 cholesky.55
  291.5 0.6 fusion.6
  292.9 0.7 fusion.17
  293.6 0.7 cholesky.44
  296.3 0.9 fusion.11
  298.3 10.0 %shard_map.124 = f32[8,128]{1,0:T(8,128)} custom-call(f32[8,128]{1,0:T(8,128)} %pad.9.x_ref), custom_call_target="tpu_custom_call" | custom-call | tf_op jit(solution)/shard_map/pallas_call | solution.py:191
  308.3 0.9 fusion.7
  309.3 0.8 convolution_add_fusion
  310.1 0.8 convolution_add_fusion.1
  (66 shorter events, 9.4 us)
Async XLA Ops:
  7.2 42.6 %copy-start = (bf16[320,320]{1,0:T(8,128)(2,1)S(1)}, bf16[320,320]{1,0:T(8,128)(2,1)}, u32[]{:S(2)}) copy-start(bf16[320,320]{1,0:T(8,128)(2,1)} %param.22) | copy-start | bytes 614404
  7.2 2.9 copy-start.5
  7.2 3.3 %copy-start.8 = (s32[512,1]{0,1:T(1,128)S(1)}, s32[512,1]{0,1:T(1,128)}, u32[]{:S(2)}) copy-start(s32[512,1]{0,1:T(1,128)} %param.21) | copy-start | bytes 6148
  7.2 80.9 %all-gather.8.cloned.1.call-start = ((), (), s32[]{:S(2)}) async-start(), calls=%async_computation.2 | async-start | bytes 4792320 | tf_op jit(solution)/shard_map/all_gather | solution.py:248
  10.0 219.8 %all-gather.6.cloned.1.call-start = ((), (), s32[]{:S(2)}) async-start(), calls=%async_computation.1 | async-start | bytes 13107200 | tf_op jit(solution)/shard_map/all_gather | solution.py:280
  161.0 0.8 copy-start.4
  237.9 31.2 %copy-start.3 = (f32[8,512]{1,0:T(8,128)S(1)}, f32[8,512]{1,0:T(8,128)}, u32[]{:S(2)}) copy-start(f32[8,512]{1,0:T(8,128)} %param.16) | copy-start | bytes 49156
  262.4 14.4 %copy-start.1 = (f32[8,512]{1,0:T(8,128)S(1)}, f32[8,512]{1,0:T(8,128)}, u32[]{:S(2)}) copy-start(f32[8,512]{1,0:T(8,128)} %param.17) | copy-start | bytes 49156
  262.4 14.4 %copy-start.7 = (f32[512]{0:T(512)S(1)}, f32[512]{0:T(512)}, u32[]{:S(2)}) copy-start(f32[512]{0:T(512)} %param.18) | copy-start | bytes 6148
  262.4 47.7 %copy-start.6 = (f32[8,512]{1,0:T(8,128)S(1)}, f32[8,512]{1,0:T(8,128)}, u32[]{:S(2)}) copy-start(f32[8,512]{1,0:T(8,128)} %param.15) | copy-start | bytes 49156
  265.8 10.7 %all-to-all-start = ((f32[8,1,4096]{2,1,0:T(1,128)}), f32[8,1,4096]{2,1,0:T(1,128)S(1)}, u32[]{:S(2)}, u32[]{:S(2)}) async-start(f32[8,1,4096]{2,1,0:T(1,128)} %all_to_all.8), calls=%async_computation | async-start | bytes 262144 | tf_op jit(solution)/shard_map/all_to_all | solution.py:301
  297.5 13.4 %copy-start.2 = (f32[8,512]{1,0:T(8,128)}, f32[8,512]{1,0:T(8,128)S(1)}, u32[]{:S(2)}) copy-start(f32[8,512]{1,0:T(8,128)S(1)} %convolution_subtract_fusion) | copy-start | bytes 49156
Sparse Core Ops, SparseCore 0:
  10.2 77.8 all-gather.7
  161.1 68.6 all-gather.5
